TPU v7x, 32 devices: a whole 2x2x4 slice. The times are simulated.
32 devices in a mesh: dp: 4 (over y, x), expert: 8 (over z, core).
Axes of the slice: x: 2, y: 2, z: 4, core: 2. Of those that a mesh axis runs over, the one named last changes fastest.
Arguments:
- tokens: bfloat16 [8192, 1280], P(('dp', 'expert')), may hold values from -6 to 6
- query_weight: bfloat16 [1280, 1280], P('dp'), may hold values from -0.15625 to 0.15625
- key_weight: bfloat16 [1280, 1280], P('dp'), may hold values from -0.15625 to 0.15625
- value_weight: bfloat16 [1280, 1280], P('dp'), may hold values from -0.15625 to 0.15625
- output_weight: bfloat16 [1280, 1280], P('dp'), may hold values from -0.625 to 0.625
- attn_gain: bfloat16 [1280], P('dp'), may hold values from 0.5 to 1.5
- ffn_gain: bfloat16 [1280], P('dp'), may hold values from 0.5 to 1.5
- router_weight: bfloat16 [1280, 16], P('dp'), may hold values from -0.078125 to 0.078125
- shared_gate: bfloat16 [1280, 896], P('dp'), may hold values from -0.15625 to 0.15625
- shared_up: bfloat16 [1280, 896], P('dp'), may hold values from -0.15625 to 0.15625
- shared_down: bfloat16 [896, 1280], P('dp'), may hold values from -0.25 to 0.25
- expert_gate: bfloat16 [16, 1280, 896], P('expert'), may hold values from -0.15625 to 0.15625
- expert_up: bfloat16 [16, 1280, 896], P('expert'), may hold values from -0.15625 to 0.15625
- expert_down: bfloat16 [16, 896, 1280], P('expert'), may hold values from -2 to 2
- expert_ids: int32 [8192, 7], P(('dp', 'expert')), may hold values from 0 to 15, all different within a row; in each aligned block of 256 rows (0 to 255, 256 to 511, ...) at most 128 rows name the same one
- piece_starts: int32 [32], P(('dp', 'expert')), may hold values from 0 to 128
- out_grad: bfloat16 [8192, 1280], P(('dp', 'expert')), may hold values from -6 to 6
Outputs:
- layer_out: bfloat16 [8192, 1280], P(('dp', 'expert'))
- tokens_grad: bfloat16 [8192, 1280], P(('dp', 'expert'))
- query_weight_grad: float32 [1280, 1280], P('dp')
- key_weight_grad: float32 [1280, 1280], P('dp')
- value_weight_grad: float32 [1280, 1280], P('dp')
- output_weight_grad: float32 [1280, 1280], P('dp')
- attn_gain_grad: float32 [1280], P('dp')
- ffn_gain_grad: float32 [1280], P('dp')
- router_weight_grad: float32 [1280, 16], P('dp')
- shared_gate_grad: float32 [1280, 896], P('dp')
- shared_up_grad: float32 [1280, 896], P('dp')
- shared_down_grad: float32 [896, 1280], P('dp')
- expert_gate_grad: float32 [16, 1280, 896], P('expert', 'dp')
- expert_up_grad: float32 [16, 1280, 896], P('expert', 'dp')
- expert_down_grad: float32 [16, 896, 1280], P('expert', 'dp')
- stat_rms: float32 [32, 3], P(('dp', 'expert'))
Inputs may be any that keep to these rules, and one draw needn't show every extreme that they name: `expert_ids`: within each sequence (aligned blocks of 256 rows) no expert is named by more than 128 rows; each row names 7 different experts. The picture piece of sequence s is tokens piece_starts[s] to piece_starts[s] + 127 of it.
All inputs are finite; a program needn't handle non-finite values.
Results may differ from a plain program's by a relative error of at most 0.023.
Values may be sent and summed in bfloat16 or wider, within the bound.
No kernel may reach another device: no remote copies, remote signals or barrier semaphores. Data moves between devices by JAX's collectives and lax.ppermute only.
A program may use at most 320 MiB of HBM per device.

v0:
```python
import jax
import jax.numpy as jnp
from jax import lax
from jax.sharding import PartitionSpec as P

HEAD_DIM = 128
TOP = 7
EXP_DEV = 2
BF = jnp.bfloat16


def product(first_arg, second_arg):
    return jnp.dot(first_arg, second_arg, preferred_element_type=jnp.float32)


def product_high(first_arg, second_arg):
    return jnp.dot(
        first_arg, second_arg, precision=lax.Precision.HIGHEST, preferred_element_type=jnp.float32
    )


def rotary_tables(length, head_size):
    half_dim = head_size // 2
    frequency = 10000.0 ** (-jnp.arange(half_dim, dtype=jnp.float32) * 2.0 / head_size)
    angles = jnp.arange(length, dtype=jnp.float32)[:, None] * frequency[None, :]
    return (jnp.cos(angles), jnp.sin(angles))


def rotate(tensor, cosine, sine_part):
    half_dim = tensor.shape[-1] // 2
    first_half = tensor[..., :half_dim]
    second_half = tensor[..., half_dim:]
    cos_rows = cosine[:, None, :]
    sin_rows = sine_part[:, None, :]
    return jnp.concatenate(
        [
            first_half * cos_rows - second_half * sin_rows,
            first_half * sin_rows + second_half * cos_rows,
        ],
        axis=-1,
    )


def allowed_mask(length, piece_start, piece_len):
    row_index = jnp.arange(length, dtype=jnp.int32)[:, None]
    col_index = jnp.arange(length, dtype=jnp.int32)[None, :]
    row_inside = (row_index >= piece_start) & (row_index < piece_start + piece_len)
    col_inside = (col_index >= piece_start) & (col_index < piece_start + piece_len)
    return (col_index <= row_index) | row_inside & col_inside


def silu_grad(inputs):
    sigmoid_part = jax.nn.sigmoid(inputs)
    return sigmoid_part * (1.0 + inputs * (1.0 - sigmoid_part))


def high_low(values):
    high = values.astype(BF)
    low = (values - high.astype(jnp.float32)).astype(BF)
    return (high, low)


def body(
    tokens,
    query_weight,
    key_weight,
    value_weight,
    output_weight,
    attn_gain,
    ffn_gain,
    router_weight,
    shared_gate,
    shared_up,
    shared_down,
    expert_gate,
    expert_up,
    expert_down,
    expert_ids,
    piece_starts,
    out_grad,
):
    dp = lax.axis_size("dp")
    owners = lax.axis_size("expert")
    me = lax.axis_index("expert")
    experts = EXP_DEV * owners
    length, width = tokens.shape
    rows = query_weight.shape[0]
    hidden = shared_gate.shape[1]
    head_count = width // HEAD_DIM
    score_scale = HEAD_DIM ** (-0.5)
    piece_len = min(256, length // 2)
    capacity = 8 * length // experts
    chosen = (expert_ids[:, :, None] == jnp.arange(experts, dtype=jnp.int32)).any(axis=1)
    chosen_low = jnp.pad(chosen.astype(BF), ((0, 0), (0, 128 - experts)))
    grads_all = lax.all_gather(
        jnp.concatenate([out_grad, chosen_low], axis=1), "expert", axis=0, tiled=True
    ).reshape(owners, length, width + 128)
    small = jnp.concatenate([router_weight, attn_gain[:, None], ffn_gain[:, None]], axis=1)
    small = jnp.pad(small, ((0, 0), (0, 128 - small.shape[1])))
    first_full = lax.all_gather(
        jnp.concatenate([query_weight, key_weight, value_weight, small], axis=1),
        "dp",
        axis=0,
        tiled=True,
    )
    second_full = lax.all_gather(
        jnp.concatenate(
            [output_weight, shared_gate, shared_up, shared_down.reshape(rows, -1)], axis=1
        ),
        "dp",
        axis=0,
        tiled=True,
    )
    query_full = first_full[:, :width]
    key_full = first_full[:, width : 2 * width]
    value_full = first_full[:, 2 * width : 3 * width]
    small_full = first_full[:, 3 * width :]
    router_full = small_full[:, :experts]
    gain_one_f = small_full[:, experts].astype(jnp.float32)
    gain_two_f = small_full[:, experts + 1].astype(jnp.float32)
    output_full = second_full[:, :width]
    shared_gate_full = second_full[:, width : width + hidden]
    shared_up_full = second_full[:, width + hidden : width + 2 * hidden]
    shared_down_full = second_full[:, width + 2 * hidden :].reshape(hidden, width)
    token_f = tokens.astype(jnp.float32)
    norm_one = lax.rsqrt(jnp.mean(token_f * token_f, axis=-1, keepdims=True) + 1e-06)
    attn_in = (token_f * norm_one * gain_one_f).astype(BF)
    cosine, sine_part = rotary_tables(length, HEAD_DIM)
    query_pre = product(attn_in, query_full).reshape(length, head_count, HEAD_DIM)
    key_pre = product(attn_in, key_full).reshape(length, head_count, HEAD_DIM)
    query_rot = rotate(query_pre, cosine, sine_part).astype(BF)
    key_rot = rotate(key_pre, cosine, sine_part).astype(BF)
    values = product(attn_in, value_full).astype(BF).reshape(length, head_count, HEAD_DIM)
    allowed = allowed_mask(length, piece_starts[0], piece_len)
    scores = (
        jnp.einsum("qhd,khd->hqk", query_rot, key_rot, preferred_element_type=jnp.float32)
        * score_scale
    )
    scores = jnp.where(allowed[None], scores, -1e30)
    row_max = jnp.max(scores, axis=-1, keepdims=True)
    exps = jnp.exp(scores - row_max)
    attn_probs = exps / jnp.sum(exps, axis=-1, keepdims=True)
    probs_low = attn_probs.astype(BF)
    context = jnp.einsum("hqk,khd->qhd", probs_low, values, preferred_element_type=jnp.float32)
    context = context.astype(BF).reshape(length, width)
    attn_out = product(context, output_full)
    residual = token_f + attn_out
    norm_two = lax.rsqrt(jnp.mean(residual * residual, axis=-1, keepdims=True) + 1e-06)
    ffn_in = (residual * norm_two * gain_two_f).astype(BF)
    router_probs = jax.nn.softmax(product(ffn_in, router_full), axis=-1)
    gates = jnp.where(chosen, router_probs, 0.0)
    gates_high, gates_low = high_low(gates)
    sent = jnp.concatenate(
        [ffn_in, gates_high, gates_low, jnp.zeros((length, 128 - 2 * experts), BF)], axis=1
    )
    rows_all = lax.all_gather(sent, "expert", axis=0, tiled=True).reshape(
        owners, length, width + 128
    )
    grad_f = out_grad.astype(jnp.float32)
    shared_gate_act = product(ffn_in, shared_gate_full)
    shared_up_act = product(ffn_in, shared_up_full)
    shared_hidden = (jax.nn.silu(shared_gate_act) * shared_up_act).astype(BF)
    shared_out = product(shared_hidden, shared_down_full)
    shared_hidden_grad = product(out_grad, shared_down_full.T)
    shared_down_grad = product(shared_hidden.T, out_grad)
    shared_gate_act_grad = (shared_hidden_grad * shared_up_act * silu_grad(shared_gate_act)).astype(
        BF
    )
    shared_up_act_grad = (shared_hidden_grad * jax.nn.silu(shared_gate_act)).astype(BF)
    shared_gate_grad = product(ffn_in.T, shared_gate_act_grad)
    shared_up_grad = product(ffn_in.T, shared_up_act_grad)
    shared_in_grad = product(shared_gate_act_grad, shared_gate_full.T) + product(
        shared_up_act_grad, shared_up_full.T
    )
    shared_parts = jnp.concatenate(
        [
            shared_gate_grad.astype(BF),
            shared_up_grad.astype(BF),
            shared_down_grad.astype(BF).reshape(dp * rows, -1),
        ],
        axis=1,
    )
    shared_share = lax.psum_scatter(shared_parts, "dp", scatter_dimension=0, tiled=True)
    own = me * EXP_DEV + jnp.arange(EXP_DEV)
    own_hot = (own[:, None] == jnp.arange(experts)[None, :]).astype(jnp.float32)
    mask = jnp.einsum(
        "ste,oe->ost", grads_all[:, :, width : width + experts].astype(jnp.float32), own_hot
    )
    slot = jnp.cumsum(mask, axis=2) - 1.0
    spread = (
        (slot[:, :, None, :] == jnp.arange(capacity, dtype=jnp.float32)[None, None, :, None])
        & (mask[:, :, None, :] > 0)
    ).astype(BF)
    gates_pair = rows_all[:, :, width : width + experts].astype(jnp.float32) + rows_all[
        :, :, width + experts : width + 2 * experts
    ].astype(jnp.float32)
    gates_own = jnp.einsum("ste,oe->ost", gates_pair, own_hot, precision=lax.Precision.HIGHEST)
    slot_gates = jnp.einsum(
        "osct,ost->osc", spread.astype(jnp.float32), gates_own, precision=lax.Precision.HIGHEST
    )
    take = lambda source: jnp.einsum(
        "osct,std->oscd", spread, source, preferred_element_type=jnp.float32
    ).astype(BF)
    expert_in = take(rows_all[:, :, :width]).reshape(EXP_DEV, owners * capacity, width)
    slot_out_grad = take(grads_all[:, :, :width])
    res_grad = (slot_gates[..., None] * slot_out_grad.astype(jnp.float32)).astype(BF)
    res_grad = res_grad.reshape(EXP_DEV, owners * capacity, width)
    mm = lambda spec, a, b: jnp.einsum(spec, a, b, preferred_element_type=jnp.float32)
    routed_gate = mm("erd,edf->erf", expert_in, expert_gate)
    routed_up = mm("erd,edf->erf", expert_in, expert_up)
    routed_hidden = (jax.nn.silu(routed_gate) * routed_up).astype(BF)
    hidden_grad = mm("erd,efd->erf", res_grad, expert_down)
    routed_gate_grad = (hidden_grad * routed_up * silu_grad(routed_gate)).astype(BF)
    routed_up_grad = (hidden_grad * jax.nn.silu(routed_gate)).astype(BF)
    expert_in_grad = (
        (
            mm("erf,edf->erd", routed_gate_grad, expert_gate)
            + mm("erf,edf->erd", routed_up_grad, expert_up)
        )
        .astype(BF)
        .reshape(EXP_DEV, owners, capacity, width)
    )
    routed_res = mm("erf,efd->erd", routed_hidden, expert_down).astype(BF)
    routed_res = routed_res.reshape(EXP_DEV, owners, capacity, width)
    slot_gate_grad = jnp.sum(
        routed_res.astype(jnp.float32) * slot_out_grad.astype(jnp.float32), axis=-1
    )
    token_gate_grad = jnp.einsum(
        "osct,osc,oe->ste",
        spread.astype(jnp.float32),
        slot_gate_grad,
        own_hot,
        precision=lax.Precision.HIGHEST,
    )
    gg_high, gg_low = high_low(token_gate_grad)
    in_grad_part = mm("osct,oscd->std", spread, expert_in_grad).astype(BF)
    back = jnp.concatenate(
        [in_grad_part, gg_high, gg_low, jnp.zeros((owners, length, 128 - 2 * experts), BF)], axis=2
    ).reshape(owners * length, width + 128)
    back = lax.psum_scatter(back, "expert", scatter_dimension=0, tiled=True)
    out_part = mm(
        "osct,oscd->std",
        (spread.astype(jnp.float32) * slot_gates[..., None]).astype(BF),
        routed_res,
    ).astype(BF)
    expert_down_part = mm("erf,erd->efd", routed_hidden, res_grad).astype(BF)
    expert_gate_part = mm("erd,erf->edf", expert_in, routed_gate_grad).astype(BF)
    expert_up_part = mm("erd,erf->edf", expert_in, routed_up_grad).astype(BF)
    expert_parts = jnp.concatenate(
        [
            expert_gate_part.reshape(EXP_DEV, dp, rows, hidden),
            expert_up_part.reshape(EXP_DEV, dp, rows, hidden),
            expert_down_part.reshape(EXP_DEV, dp, rows, hidden),
        ],
        axis=0,
    ).transpose(1, 0, 2, 3)
    expert_share = lax.psum_scatter(expert_parts, "dp", scatter_dimension=0, tiled=True)[0]
    expert_share = expert_share.astype(jnp.float32)
    out_sum = lax.psum_scatter(
        out_part.reshape(owners * length, width), "expert", scatter_dimension=0, tiled=True
    )
    routed_in_grad = back[:, :width].astype(jnp.float32)
    probs_grad = back[:, width : width + experts].astype(jnp.float32) + back[
        :, width + experts : width + 2 * experts
    ].astype(jnp.float32)
    logits_grad = router_probs * (
        probs_grad - jnp.sum(router_probs * probs_grad, axis=-1, keepdims=True)
    )
    router_grad = product_high(ffn_in.astype(jnp.float32).T, logits_grad)
    router_in_grad = product_high(logits_grad, router_full.astype(jnp.float32).T)
    ffn_in_grad = shared_in_grad + routed_in_grad + router_in_grad
    ffn_gain_grad = jnp.sum(ffn_in_grad * residual * norm_two, axis=0)
    upstream_two = ffn_in_grad * gain_two_f
    residual_grad = (
        grad_f
        + norm_two * upstream_two
        - residual * norm_two**3 * jnp.mean(upstream_two * residual, axis=-1, keepdims=True)
    )
    attn_out_grad = residual_grad.astype(BF)
    output_grad = product(context.T, attn_out_grad)
    context_grad = (
        product(attn_out_grad, output_full.T).astype(BF).reshape(length, head_count, HEAD_DIM)
    )
    value_grad = mm("hqk,qhd->khd", probs_low, context_grad).astype(BF).reshape(length, width)
    probs_grad_att = mm("qhd,khd->hqk", context_grad, values)
    row_delta = jnp.sum(attn_probs * probs_grad_att, axis=-1, keepdims=True)
    scores_grad = (attn_probs * (probs_grad_att - row_delta)).astype(BF)
    query_grad = mm("hqk,khd->qhd", scores_grad, key_rot) * score_scale
    key_grad = mm("hqk,qhd->khd", scores_grad, query_rot) * score_scale
    query_pre_grad = rotate(query_grad, cosine, -sine_part).astype(BF).reshape(length, width)
    key_pre_grad = rotate(key_grad, cosine, -sine_part).astype(BF).reshape(length, width)
    query_wgrad = product(attn_in.T, query_pre_grad)
    key_wgrad = product(attn_in.T, key_pre_grad)
    value_wgrad = product(attn_in.T, value_grad)
    attn_in_grad = (
        product(query_pre_grad, query_full.T)
        + product(key_pre_grad, key_full.T)
        + product(value_grad, value_full.T)
    )
    attn_gain_grad = jnp.sum(attn_in_grad * token_f * norm_one, axis=0)
    upstream_one = attn_in_grad * gain_one_f
    tokens_grad = (
        residual_grad
        + norm_one * upstream_one
        - token_f * norm_one**3 * jnp.mean(upstream_one * token_f, axis=-1, keepdims=True)
    )
    small_grads = jnp.concatenate(
        [router_grad, attn_gain_grad[:, None], ffn_gain_grad[:, None]], axis=1
    ).astype(BF)
    small_grads = jnp.pad(small_grads, ((0, 0), (0, 128 - small_grads.shape[1])))
    attn_parts = jnp.concatenate(
        [
            query_wgrad.astype(BF),
            key_wgrad.astype(BF),
            value_wgrad.astype(BF),
            output_grad.astype(BF),
            small_grads,
        ],
        axis=1,
    )
    attn_share = lax.psum_scatter(attn_parts, "dp", scatter_dimension=0, tiled=True)
    shared_share = lax.psum(shared_share, "expert").astype(jnp.float32)
    attn_share = lax.psum(attn_share, "expert").astype(jnp.float32)
    moe_out = shared_out + out_sum.astype(jnp.float32)
    stream_out = residual + moe_out
    stat_rms = jnp.stack(
        [
            jnp.sqrt(jnp.mean(attn_out * attn_out)),
            jnp.sqrt(jnp.mean(moe_out * moe_out)),
            jnp.sqrt(jnp.mean(stream_out * stream_out)),
        ]
    )[None, :]
    return (
        stream_out.astype(BF),
        tokens_grad.astype(BF),
        attn_share[:, :width],
        attn_share[:, width : 2 * width],
        attn_share[:, 2 * width : 3 * width],
        attn_share[:, 3 * width : 4 * width],
        attn_share[:, 4 * width + experts],
        attn_share[:, 4 * width + experts + 1],
        attn_share[:, 4 * width : 4 * width + experts],
        shared_share[:, :hidden],
        shared_share[:, hidden : 2 * hidden],
        shared_share[:, 2 * hidden :].reshape(shared_down.shape),
        expert_share[0:2],
        expert_share[2:4],
        expert_share[4:6].reshape(EXP_DEV, shared_down.shape[0], width),
        stat_rms,
    )


def solution(mesh):
    in_specs = (
        P(("dp", "expert"), None),
        P("dp", None),
        P("dp", None),
        P("dp", None),
        P("dp", None),
        P("dp"),
        P("dp"),
        P("dp", None),
        P("dp", None),
        P("dp", None),
        P("dp", None),
        P("expert", None, None),
        P("expert", None, None),
        P("expert", None, None),
        P(("dp", "expert"), None),
        P(("dp", "expert")),
        P(("dp", "expert"), None),
    )
    out_specs = (
        P(("dp", "expert"), None),
        P(("dp", "expert"), None),
        P("dp", None),
        P("dp", None),
        P("dp", None),
        P("dp", None),
        P("dp"),
        P("dp"),
        P("dp", None),
        P("dp", None),
        P("dp", None),
        P("dp", None),
        P("expert", "dp", None),
        P("expert", "dp", None),
        P("expert", "dp", None),
        P(("dp", "expert"), None),
    )
    return jax.shard_map(body, mesh=mesh, in_specs=in_specs, out_specs=out_specs, check_vma=False)
```

profile of v0, /device:TPU:0, one launch (start us, length us, event | category | flops | bytes accessed | tf_op | source)
XLA Modules:
  0.0 1105.5 jit_solution(541754291438317677)
XLA Ops:
  21.2 96.2 %all-gather.5.cloned.1.call-done = bf16[1280,3968]{1,0:T(8,128)(2,1)} async-done(((bf16[320,3968]{1,0:T(8,128)(2,1)}), bf16[1280,3968]{1,0:T(8,128)(2,1)}) %all-gather.5.cloned.1.call-update) | async-done | bytes 10158096 | tf_op jit(solution)/shard_map/all_gather | solution.py:100
  151.9 69.7 %all-gather.7.cloned.1.call-done = bf16[1280,3968]{1,0:T(8,128)(2,1)} async-done(((bf16[320,3968]{1,0:T(8,128)(2,1)}), bf16[1280,3968]{1,0:T(8,128)(2,1)}) %all-gather.7.cloned.1.call-update) | async-done | bytes 10158096 | tf_op jit(solution)/shard_map/all_gather | solution.py:106
  230.1 54.0 %all-gather.9.cloned.1.call-done = bf16[2048,1408]{1,0:T(8,128)(2,1)} async-done(((bf16[256,1408]{1,0:T(8,128)(2,1)}), bf16[2048,1408]{1,0:T(8,128)(2,1)}) %all-gather.9.cloned.1.call-update) | async-done | bytes 5767184 | tf_op jit(solution)/shard_map/all_gather | solution.py:95
  286.9 58.7 %all-gather.11.cloned.1.call-done = bf16[2048,1408]{0,1:T(8,128)(2,1)} async-done(((bf16[256,1408]{0,1:T(8,128)(2,1)}), bf16[2048,1408]{0,1:T(8,128)(2,1)}) %all-gather.11.cloned.1.call-update) | async-done | bytes 5767184 | tf_op jit(solution)/shard_map/all_gather | solution.py:156
  345.7 5.1 copy.343
  356.1 5.1 fusion.1
  364.0 8.6 copy.341
  377.7 11.8 %fusion.136 = f32[2,1024,896]{2,1,0:T(8,128)} fusion(bf16[2,1024,1280]{2,1,0:T(8,128)(2,1)S(1)} %bitcast.159, bf16[2,1280,896]{2,1,0:T(8,128)(2,1)} %param.28), kind=kOutput, calls=%fused_computation.225 | convolution fusion | flops 4697620480 | bytes 17170432 | tf_op jit(solution)/shard_map/erd,edf->erf/dot_general | solution.py:208
  389.6 7.6 fusion.137
  397.2 14.7 %multiply_convert_fusion = (bf16[2,1024,896]{2,1,0:T(8,128)(2,1)}, bf16[2,1024,896]{2,1,0:T(8,128)(2,1)}, bf16[2,1024,896]{2,1,0:T(8,128)(2,1)}) fusion(f32[2,1024,896]{2,1,0:T(8,128)} %fusion.136, f32[2,1024,896]{2,1,0:T(8,128)} %fusion.137, bf16[2,1024,1280]{2,1,0:T(8,128)(2,1)} %bitcast.163, bf16[2,896,1280]{2,1,0:T(8,128)(2,1)S(1)} %bitcast.194), kind=kOutput, calls=%fused_computation.18 | convolution fusion | flops 4725145600 | bytes 35520512 | tf_op jit(solution)/shard_map/erd,efd->erf/dot_general | solution.py:208
  412.0 7.5 convolution_convert_fusion.5
  425.1 11.4 %fusion.138 = f32[2,1024,1280]{2,1,0:T(8,128)} fusion(bf16[2,1024,896]{2,1,0:T(8,128)(2,1)} %get-tuple-element.115, bf16[2,1280,896]{2,1,0:T(8,128)(2,1)} %param.28), kind=kOutput, calls=%fused_computation.227 | convolution fusion | flops 4697620480 | bytes 18743296 | tf_op jit(solution)/shard_map/erf,edf->erd/dot_general | solution.py:208
  436.5 9.9 add_convert_fusion
  450.5 10.0 concatenate.54
  460.5 8.2 copy.328
  468.7 5.2 bitcast_convert_fusion.1
  473.9 7.9 copy.327
  506.9 5.6 pad_maximum_fusion.1
  512.6 10.0 copy.332
  537.1 55.2 %reduce-scatter.12.cloned.1.call-done = bf16[256,1280]{0,1:T(8,128)(2,1)} async-done(((bf16[2048,1280]{0,1:T(8,128)(2,1)}), bf16[256,1280]{0,1:T(8,128)(2,1)}) %reduce-scatter.12.cloned.1.call-update) | async-done | bytes 655376 | tf_op jit(solution)/shard_map/reduce_scatter | solution.py:259
  592.3 4.9 multiply_reduce_fusion.2
  638.7 18.6 %copy.330 = bf16[1280,5248]{1,0:T(8,128)(2,1)} copy(bf16[1280,5248]{0,1:T(8,128)(2,1)} %fusion.84) | data formatting | bytes 26869760
  657.3 10.8 convolution_convert_fusion.7
  668.1 9.1 reshape.335
  677.2 10.0 convolution_convert_fusion.9
  687.2 8.4 convolution_convert_fusion.8
  695.7 6.9 copy_bitcast_fusion
  707.0 92.5 %reduce-scatter.16.cloned.1.call-done = bf16[320,5248]{1,0:T(8,128)(2,1)} async-done(((bf16[1280,5248]{1,0:T(8,128)(2,1)}), bf16[320,5248]{1,0:T(8,128)(2,1)}) %reduce-scatter.16.cloned.1.call-update) | async-done | bytes 3358736
  799.5 6.1 copy.331
  812.3 120.6 %reduce-scatter.20.cloned.1.call-done = bf16[1,6,320,896]{3,2,1,0:T(8,128)(2,1)} async-done(((bf16[4,6,320,896]{3,2,1,0:T(8,128)(2,1)}), bf16[1,6,320,896]{3,2,1,0:T(8,128)(2,1)}) %reduce-scatter.20.cloned.1.call-update) | async-done | bytes 3440656
  941.7 125.9 %all-reduce.7.cloned.1.call-done = (bf16[320,2688]{0,1:T(8,128)(2,1)}, bf16[320,5248]{0,1:T(8,128)(2,1)}) async-done(((bf16[320,2688]{0,1:T(8,128)(2,1)}, bf16[320,5248]{0,1:T(8,128)(2,1)}), (bf16[320,2688]{0,1:T(8,128)(2,1)}, bf16[320,5248]{0,1:T(8,128)(2,1)})) %all-reduce.7.cloned.1.call-update) | async-done | bytes 5079056 | tf_op jit(solution)/shard_map/psum | solution.py:322
  1067.6 5.0 fusion.130
  (298 shorter events, 205.9 us)
Async XLA Ops:
  7.2 110.3 %all-gather.5.cloned.1.call-start = ((), (), s32[]{:S(2)}) async-start(), calls=%async_computation.5 | async-start | bytes 12697600 | tf_op jit(solution)/shard_map/all_gather | solution.py:100
  12.4 209.2 %all-gather.7.cloned.1.call-start = ((), (), s32[]{:S(2)}) async-start(), calls=%async_computation.6 | async-start | bytes 12697600 | tf_op jit(solution)/shard_map/all_gather | solution.py:106
  15.5 268.7 %all-gather.9.cloned.1.call-start = ((), (), s32[]{:S(2)}) async-start(), calls=%async_computation.7 | async-start | bytes 6488064 | tf_op jit(solution)/shard_map/all_gather | solution.py:95
  17.5 328.2 %all-gather.11.cloned.1.call-start = ((), (), s32[]{:S(2)}) async-start(), calls=%async_computation.8 | async-start | bytes 6488064 | tf_op jit(solution)/shard_map/all_gather | solution.py:156
  17.8 208.1 %copy-start.3 = (bf16[256,1280]{0,1:T(8,128)(2,1)}, bf16[256,1280]{0,1:T(8,128)(2,1)S(1)}, u32[]{:S(2)}) copy-start(bf16[256,1280]{0,1:T(8,128)(2,1)S(1)} %copy.227) | copy-start | bytes 1966084
  19.3 103.2 %copy-start.53 = (f32[256]{0:T(256)}, f32[256]{0:T(256)S(1)}, u32[]{:S(2)}) copy-start(f32[256]{0:T(256)S(1)} %get-tuple-element.151) | copy-start | bytes 3076
  21.2 120.9 %copy-start.24 = (f32[256,64]{1,0:T(8,128)}, f32[256,64]{1,0:T(8,128)S(1)}, u32[]{:S(2)}) copy-start(f32[256,64]{1,0:T(8,128)S(1)} %get-tuple-element.156) | copy-start | bytes 196612
  119.0 107.7 %copy-start.42 = (f32[1280]{0:T(1024)}, f32[1280]{0:T(1024)S(1)}, u32[]{:S(2)}) copy-start(f32[1280]{0:T(1024)S(1)} %get-tuple-element.96) | copy-start | bytes 15364
  229.9 301.9 %reduce-scatter.14.cloned.1.call-start = ((), (), s32[]{:S(2)}) async-start(), calls=%async_computation.10 | async-start | bytes 6488064 | tf_op jit(solution)/shard_map/reduce_scatter | solution.py:240
  377.2 12.4 %slice-start.12 = ((s8[4587520]{0:T(1024)(128)(4,1)}), s8[393216]{0:T(1024)(128)(4,1)S(1)}, s32[]{:S(2)}) async-start(s8[4587520]{0:T(1024)(128)(4,1)} %bitcast.195), calls=%async_computation.27 | async-start | bytes 786432
  377.7 11.9 %copy-start.12 = (bf16[2,8,128,1280]{3,2,1,0:T(8,128)(2,1)}, bf16[2,8,128,1280]{3,2,1,0:T(8,128)(2,1)S(1)}, u32[]{:S(2)}) copy-start(bf16[2,8,128,1280]{3,2,1,0:T(8,128)(2,1)S(1)} %copy.246) | copy-start | bytes 15728644
  377.7 11.9 %slice-start.13 = ((s8[4587520]{0:T(1024)(128)(4,1)}), s8[4194304]{0:T(1024)(128)(4,1)S(1)}, s32[]{:S(2)}) async-start(s8[4587520]{0:T(1024)(128)(4,1)} %bitcast.195), calls=%async_computation.28 | async-start | bytes 8388608
  377.7 19.5 %slice-start.10 = ((s8[4587520]{0:T(1024)(128)(4,1)}), s8[4194304]{0:T(1024)(128)(4,1)S(1)}, s32[]{:S(2)}) async-start(s8[4587520]{0:T(1024)(128)(4,1)} %bitcast.193), calls=%async_computation.25 | async-start | bytes 8388608
  389.6 7.7 slice-start.11
  412.0 7.5 slice-start.3
  412.0 7.5 slice-start.4
  425.1 11.4 %copy-start.55 = (bf16[2,1024,896]{2,1,0:T(8,128)(2,1)S(1)}, bf16[2,1024,896]{2,1,0:T(8,128)(2,1)}, u32[]{:S(2)}) copy-start(bf16[2,1024,896]{2,1,0:T(8,128)(2,1)} %get-tuple-element.114) | copy-start | bytes 11010052
  468.7 123.6 %reduce-scatter.12.cloned.1.call-start = ((), (), s32[]{:S(2)}) async-start(), calls=%async_computation.9 | async-start | bytes 5898240 | tf_op jit(solution)/shard_map/reduce_scatter | solution.py:259
  481.9 221.1 %reduce-scatter.18.cloned.1.call-start = ((), (), s32[]{:S(2)}) async-start(), calls=%async_computation.12 | async-start | bytes 8601600
  522.6 276.9 %reduce-scatter.16.cloned.1.call-start = ((), (), s32[]{:S(2)}) async-start(), calls=%async_computation.11 | async-start | bytes 16793600
  535.2 57.0 %copy-start.2 = (f32[256,1280]{0,1:T(8,128)S(1)}, f32[256,1280]{0,1:T(8,128)}, u32[]{:S(2)}) copy-start(f32[256,1280]{0,1:T(8,128)} %copy-done.1) | copy-start | bytes 3932164
  535.3 57.0 %copy-start.43 = (f32[1280]{0:T(1024)S(1)}, f32[1280]{0:T(1024)}, u32[]{:S(2)}) copy-start(f32[1280]{0:T(1024)} %copy-done.42) | copy-start | bytes 15364
  535.3 57.0 %copy-start.49 = (f32[256]{0:T(256)S(1)}, f32[256]{0:T(256)}, u32[]{:S(2)}) copy-start(f32[256]{0:T(256)} %copy-done.48) | copy-start | bytes 3076
  537.1 60.1 %copy-start.11 = (f32[256,1280]{0,1:T(8,128)}, f32[256,1280]{0,1:T(8,128)S(1)}, u32[]{:S(2)}) copy-start(f32[256,1280]{0,1:T(8,128)S(1)} %convolution_add_fusion) | copy-start | bytes 3932164
  537.1 60.1 %copy-start.51 = (f32[256]{0:T(256)S(1)}, f32[256]{0:T(256)}, u32[]{:S(2)}) copy-start(f32[256]{0:T(256)} %get-tuple-element.152) | copy-start | bytes 3076
  598.9 5.8 copy-start.28
  614.2 7.5 slice-start.5
  657.3 275.6 %reduce-scatter.20.cloned.1.call-start = ((), (), s32[]{:S(2)}) async-start(), calls=%async_computation.13 | async-start | bytes 17203200
  677.2 10.0 copy-start.56
  677.2 18.4 %slice-start = ((s8[4587520]{0:T(1024)(128)(4,1)}), s8[4194304]{0:T(1024)(128)(4,1)S(1)}, s32[]{:S(2)}) async-start(s8[4587520]{0:T(1024)(128)(4,1)} %bitcast.156), calls=%async_computation.15 | async-start | bytes 8388608
  687.2 8.5 slice-start.1
  702.7 364.9 %all-reduce.7.cloned.1.call-start = ((), (), s32[]{:S(2)}) async-start(), calls=%async_computation.14 | async-start | bytes 12189696 | tf_op jit(solution)/shard_map/psum | solution.py:322
  (49 other events, 130.3 us)
Sparse Core Ops, SparseCore 0:
  12.5 104.9 all-gather.4
  119.3 102.1 all-gather.6
  223.7 60.3 all-gather.8
  286.1 59.4 all-gather.10
  468.8 62.9 reduce-scatter.13
  534.0 58.2 reduce-scatter.11
  595.3 73.4 reduce-scatter.17
  672.0 127.5 reduce-scatter.15
  802.6 130.2 reduce-scatter.19
  935.2 132.3 all-reduce.6
where the time goes:
time: 1120 us; the launch traced here: 1110 us
  waiting for transfers between devices  677 us (60%)
  matrix products  195 us (17%)
  local copies, waits for them, and re-layouts  170 us (15%)
  other arithmetic  43.5 us (4%)
  between operations  18.3 us (2%)
    unnamed x13, waiting for transfers between devices  213 us
    psum x1, waiting for transfers between devices, body(): shared_share = lax.psum(shared_share, 'expert').astype(jnp.float32)  126 us
    dot_general x15, matrix products, body(): jnp.einsum(spec, a, b, preferred_element_type=jnp.float32)  106 us
    all_gather x1, waiting for transfers between devices, body(): lax.all_gather(jnp.concatenate([query_weight, key_weight, value_weight, s...  96.2 us
    unnamed x161, local copies, waits for them, and re-layouts  83.6 us
    all_gather x1, waiting for transfers between devices, body(): lax.all_gather(jnp.concatenate([output_weight, shared_gate, shared_up, sh...  69.7 us
    dot_general x22, matrix products, product(): return jnp.dot(first_arg, second_arg, preferred_element_type=jnp.float32)  64 us
    all_gather x1, waiting for transfers between devices, body(): lax.all_gather(sent, 'expert', axis=0, tiled=True)  58.7 us
  transfers between devices with their start and end apart: 10, of which 9 were waited for; matrix products, arithmetic and copies ran while one was open for 22% of the time, Pallas kernels for 0%

commit v1 on v0

--- a/solution.py
+++ b/solution.py
@@ -319,7 +319,7 @@
         axis=1,
     )
     attn_share = lax.psum_scatter(attn_parts, "dp", scatter_dimension=0, tiled=True)
-    shared_share = lax.psum(shared_share, "expert").astype(jnp.float32)
+    shared_share = jnp.sum(lax.all_gather(shared_share, "expert"), axis=0).astype(jnp.float32)
     attn_share = lax.psum(attn_share, "expert").astype(jnp.float32)
     moe_out = shared_out + out_sum.astype(jnp.float32)
     stream_out = residual + moe_out

time: 1120 us -> 1190 us (1.062)
  waiting for transfers between devices: 677 us -> 759 us
  local copies, waits for them, and re-layouts: 170 us -> 158 us
    all_gather x0 -> x1, waiting for transfers between devices: none -> 119 us  [body(): lax.all_gather(shared_share, 'expert')]
    psum x1, waiting for transfers between devices: 126 us -> 83.7 us  [body(): attn_share = lax.psum(attn_share, 'expert').astype(jnp.float32)]
    unnamed x161 -> x152, local copies, waits for them, and re-layouts: 83.6 us -> 76.4 us
  transfers between devices with their start and end apart: 10 -> 11, of which waited for: 9 -> 10; matrix products, arithmetic and copies ran while one was open for 22% -> 21% of each run, Pallas kernels for 0% -> 0%
where the time goes in v1:
time: 1190 us; the launch traced here: 1180 us
  waiting for transfers between devices  759 us (64%)
  matrix products  195 us (16%)
  local copies, waits for them, and re-layouts  158 us (13%)
  other arithmetic  50.4 us (4%)
  between operations  18 us (2%)
    unnamed x13, waiting for transfers between devices  217 us
    all_gather x1, waiting for transfers between devices, body(): lax.all_gather(shared_share, 'expert')  119 us
    dot_general x15, matrix products, body(): jnp.einsum(spec, a, b, preferred_element_type=jnp.float32)  106 us
    all_gather x1, waiting for transfers between devices, body(): lax.all_gather(jnp.concatenate([query_weight, key_weight, value_weight, s...  96.3 us
    psum x1, waiting for transfers between devices, body(): attn_share = lax.psum(attn_share, 'expert').astype(jnp.float32)  83.7 us
    unnamed x152, local copies, waits for them, and re-layouts  76.4 us
    all_gather x1, waiting for transfers between devices, body(): lax.all_gather(jnp.concatenate([output_weight, shared_gate, shared_up, sh...  69.6 us
    dot_general x22, matrix products, product(): return jnp.dot(first_arg, second_arg, preferred_element_type=jnp.float32)  64 us
  transfers between devices with their start and end apart: 11, of which 10 were waited for; matrix products, arithmetic and copies ran while one was open for 21% of the time, Pallas kernels for 0%

profile of v1, /device:TPU:0, one launch (start us, length us, event | category | flops | bytes accessed | tf_op | source)
XLA Modules:
  0.0 1181.4 jit_solution(5277755415116283899)
XLA Ops:
  21.2 96.3 %all-gather.7.cloned.1.call-done = bf16[1280,3968]{1,0:T(8,128)(2,1)} async-done(((bf16[320,3968]{1,0:T(8,128)(2,1)}), bf16[1280,3968]{1,0:T(8,128)(2,1)}) %all-gather.7.cloned.1.call-update) | async-done | bytes 10158096 | tf_op jit(solution)/shard_map/all_gather | solution.py:100
  151.9 69.6 %all-gather.9.cloned.1.call-done = bf16[1280,3968]{1,0:T(8,128)(2,1)} async-done(((bf16[320,3968]{1,0:T(8,128)(2,1)}), bf16[1280,3968]{1,0:T(8,128)(2,1)}) %all-gather.9.cloned.1.call-update) | async-done | bytes 10158096 | tf_op jit(solution)/shard_map/all_gather | solution.py:106
  230.1 54.0 %all-gather.11.cloned.1.call-done = bf16[2048,1408]{1,0:T(8,128)(2,1)} async-done(((bf16[256,1408]{1,0:T(8,128)(2,1)}), bf16[2048,1408]{1,0:T(8,128)(2,1)}) %all-gather.11.cloned.1.call-update) | async-done | bytes 5767184 | tf_op jit(solution)/shard_map/all_gather | solution.py:95
  286.9 58.7 %all-gather.13.cloned.1.call-done = bf16[2048,1408]{0,1:T(8,128)(2,1)} async-done(((bf16[256,1408]{0,1:T(8,128)(2,1)}), bf16[2048,1408]{0,1:T(8,128)(2,1)}) %all-gather.13.cloned.1.call-update) | async-done | bytes 5767184 | tf_op jit(solution)/shard_map/all_gather | solution.py:156
  345.7 5.1 copy.333
  356.1 5.1 fusion.1
  363.9 8.7 copy.331
  377.7 11.8 fusion.136
  389.5 7.6 fusion.137
  397.2 14.7 %multiply_convert_fusion = (bf16[2,1024,896]{2,1,0:T(8,128)(2,1)}, bf16[2,1024,896]{2,1,0:T(8,128)(2,1)}, bf16[2,1024,896]{2,1,0:T(8,128)(2,1)}) fusion(f32[2,1024,896]{2,1,0:T(8,128)} %fusion.136, f32[2,1024,896]{2,1,0:T(8,128)} %fusion.137, bf16[2,1024,1280]{2,1,0:T(8,128)(2,1)} %bitcast.165, bf16[2,896,1280]{2,1,0:T(8,128)(2,1)S(1)} %bitcast.196), kind=kOutput, calls=%fused_computation.18 | convolution fusion | flops 4725145600 | bytes 35520512 | tf_op jit(solution)/shard_map/erd,efd->erf/dot_general | solution.py:208
  411.9 7.5 convolution_convert_fusion.5
  425.1 11.3 fusion.138
  436.4 9.9 add_convert_fusion
  450.5 10.0 concatenate.54
  460.5 8.2 copy.318
  468.8 5.2 bitcast_convert_fusion.1
  473.9 7.9 copy.317
  507.0 5.7 pad_maximum_fusion.1
  512.7 9.8 copy.322
  537.1 55.2 %reduce-scatter.12.cloned.1.call-done = bf16[256,1280]{0,1:T(8,128)(2,1)} async-done(((bf16[2048,1280]{0,1:T(8,128)(2,1)}), bf16[256,1280]{0,1:T(8,128)(2,1)}) %reduce-scatter.12.cloned.1.call-update) | async-done | bytes 655376 | tf_op jit(solution)/shard_map/reduce_scatter | solution.py:259
  638.7 18.5 %copy.320 = bf16[1280,5248]{1,0:T(8,128)(2,1)} copy(bf16[1280,5248]{0,1:T(8,128)(2,1)} %fusion.84) | data formatting | bytes 26869760
  657.2 10.9 convolution_convert_fusion.7
  668.1 9.1 reshape.335
  677.2 10.0 convolution_convert_fusion.9
  687.2 8.5 convolution_convert_fusion.8
  695.7 6.9 copy_bitcast_fusion
  703.5 96.1 %reduce-scatter.16.cloned.1.call-done = bf16[320,5248]{1,0:T(8,128)(2,1)} async-done(((bf16[1280,5248]{1,0:T(8,128)(2,1)}), bf16[320,5248]{1,0:T(8,128)(2,1)}) %reduce-scatter.16.cloned.1.call-update) | async-done | bytes 3358736
  799.6 6.1 copy.321
  812.4 120.6 %reduce-scatter.20.cloned.1.call-done = bf16[1,6,320,896]{3,2,1,0:T(8,128)(2,1)} async-done(((bf16[4,6,320,896]{3,2,1,0:T(8,128)(2,1)}), bf16[1,6,320,896]{3,2,1,0:T(8,128)(2,1)}) %reduce-scatter.20.cloned.1.call-update) | async-done | bytes 3440656
  941.7 119.1 %all-gather.15.cloned.1.call-done = bf16[2560,2688]{1,0:T(8,128)(2,1)} async-done(((bf16[320,2688]{1,0:T(8,128)(2,1)}), bf16[2560,2688]{1,0:T(8,128)(2,1)}) %all-gather.15.cloned.1.call-update) | async-done | bytes 13762576 | tf_op jit(solution)/shard_map/all_gather | solution.py:322
  1060.9 7.8 reduce_sum.149
  1071.6 83.7 %all-reduce.6.cloned.1.call-done = bf16[320,5248]{0,1:T(8,128)(2,1)} async-done(((bf16[320,5248]{0,1:T(8,128)(2,1)}), bf16[320,5248]{0,1:T(8,128)(2,1)}) %all-reduce.6.cloned.1.call-update) | async-done | bytes 3358736 | tf_op jit(solution)/shard_map/psum | solution.py:323
  (292 shorter events, 203.6 us)
Async XLA Ops:
  7.2 110.3 %all-gather.7.cloned.1.call-start = ((), (), s32[]{:S(2)}) async-start(), calls=%async_computation.5 | async-start | bytes 12697600 | tf_op jit(solution)/shard_map/all_gather | solution.py:100
  12.4 209.2 %all-gather.9.cloned.1.call-start = ((), (), s32[]{:S(2)}) async-start(), calls=%async_computation.6 | async-start | bytes 12697600 | tf_op jit(solution)/shard_map/all_gather | solution.py:106
  15.5 268.7 %all-gather.11.cloned.1.call-start = ((), (), s32[]{:S(2)}) async-start(), calls=%async_computation.7 | async-start | bytes 6488064 | tf_op jit(solution)/shard_map/all_gather | solution.py:95
  17.5 328.2 %all-gather.13.cloned.1.call-start = ((), (), s32[]{:S(2)}) async-start(), calls=%async_computation.8 | async-start | bytes 6488064 | tf_op jit(solution)/shard_map/all_gather | solution.py:156
  17.8 208.1 %copy-start.2 = (bf16[256,1280]{0,1:T(8,128)(2,1)}, bf16[256,1280]{0,1:T(8,128)(2,1)S(1)}, u32[]{:S(2)}) copy-start(bf16[256,1280]{0,1:T(8,128)(2,1)S(1)} %copy.219) | copy-start | bytes 1966084
  19.3 103.3 %copy-start.50 = (f32[256]{0:T(256)}, f32[256]{0:T(256)S(1)}, u32[]{:S(2)}) copy-start(f32[256]{0:T(256)S(1)} %get-tuple-element.149) | copy-start | bytes 3076
  21.2 121.0 %copy-start.21 = (f32[256,64]{1,0:T(8,128)}, f32[256,64]{1,0:T(8,128)S(1)}, u32[]{:S(2)}) copy-start(f32[256,64]{1,0:T(8,128)S(1)} %get-tuple-element.154) | copy-start | bytes 196612
  119.1 107.7 %copy-start.39 = (f32[1280]{0:T(1024)}, f32[1280]{0:T(1024)S(1)}, u32[]{:S(2)}) copy-start(f32[1280]{0:T(1024)S(1)} %get-tuple-element.96) | copy-start | bytes 15364
  229.9 302.0 %reduce-scatter.14.cloned.1.call-start = ((), (), s32[]{:S(2)}) async-start(), calls=%async_computation.10 | async-start | bytes 6488064 | tf_op jit(solution)/shard_map/reduce_scatter | solution.py:240
  377.1 12.3 %slice-start.12 = ((s8[4587520]{0:T(1024)(128)(4,1)}), s8[393216]{0:T(1024)(128)(4,1)S(1)}, s32[]{:S(2)}) async-start(s8[4587520]{0:T(1024)(128)(4,1)} %bitcast.197), calls=%async_computation.28 | async-start | bytes 786432
  377.7 11.8 %copy-start.9 = (bf16[2,8,128,1280]{3,2,1,0:T(8,128)(2,1)}, bf16[2,8,128,1280]{3,2,1,0:T(8,128)(2,1)S(1)}, u32[]{:S(2)}) copy-start(bf16[2,8,128,1280]{3,2,1,0:T(8,128)(2,1)S(1)} %copy.238) | copy-start | bytes 15728644
  377.7 11.8 %slice-start.13 = ((s8[4587520]{0:T(1024)(128)(4,1)}), s8[4194304]{0:T(1024)(128)(4,1)S(1)}, s32[]{:S(2)}) async-start(s8[4587520]{0:T(1024)(128)(4,1)} %bitcast.197), calls=%async_computation.29 | async-start | bytes 8388608
  377.7 19.5 %slice-start.10 = ((s8[4587520]{0:T(1024)(128)(4,1)}), s8[4194304]{0:T(1024)(128)(4,1)S(1)}, s32[]{:S(2)}) async-start(s8[4587520]{0:T(1024)(128)(4,1)} %bitcast.195), calls=%async_computation.26 | async-start | bytes 8388608
  389.5 7.7 slice-start.11
  411.9 7.5 slice-start.3
  411.9 7.5 slice-start.4
  425.1 11.3 copy-start.52
  468.7 123.6 %reduce-scatter.12.cloned.1.call-start = ((), (), s32[]{:S(2)}) async-start(), calls=%async_computation.9 | async-start | bytes 5898240 | tf_op jit(solution)/shard_map/reduce_scatter | solution.py:259
  481.9 220.8 %reduce-scatter.18.cloned.1.call-start = ((), (), s32[]{:S(2)}) async-start(), calls=%async_computation.14 | async-start | bytes 8601600 | tf_op jit(solution)/shard_map/reduce_scatter | solution.py:183
  522.5 277.0 %reduce-scatter.16.cloned.1.call-start = ((), (), s32[]{:S(2)}) async-start(), calls=%async_computation.13 | async-start | bytes 16793600
  535.3 57.1 %copy-start.1 = (f32[256,1280]{0,1:T(8,128)S(1)}, f32[256,1280]{0,1:T(8,128)}, u32[]{:S(2)}) copy-start(f32[256,1280]{0,1:T(8,128)} %copy-done) | copy-start | bytes 3932164
  535.3 57.1 %copy-start.40 = (f32[1280]{0:T(1024)S(1)}, f32[1280]{0:T(1024)}, u32[]{:S(2)}) copy-start(f32[1280]{0:T(1024)} %copy-done.39) | copy-start | bytes 15364
  535.3 57.1 %copy-start.46 = (f32[256]{0:T(256)S(1)}, f32[256]{0:T(256)}, u32[]{:S(2)}) copy-start(f32[256]{0:T(256)} %copy-done.45) | copy-start | bytes 3076
  537.1 60.1 %copy-start.8 = (f32[256,1280]{0,1:T(8,128)}, f32[256,1280]{0,1:T(8,128)S(1)}, u32[]{:S(2)}) copy-start(f32[256,1280]{0,1:T(8,128)S(1)} %convolution_add_fusion) | copy-start | bytes 3932164
  537.1 60.1 %copy-start.48 = (f32[256]{0:T(256)S(1)}, f32[256]{0:T(256)}, u32[]{:S(2)}) copy-start(f32[256]{0:T(256)} %get-tuple-element.150) | copy-start | bytes 3076
  614.3 7.5 slice-start.5
  657.2 275.8 %reduce-scatter.20.cloned.1.call-start = ((), (), s32[]{:S(2)}) async-start(), calls=%async_computation.15 | async-start | bytes 17203200
  677.2 10.0 copy-start.53
  677.2 18.5 %slice-start = ((s8[4587520]{0:T(1024)(128)(4,1)}), s8[4194304]{0:T(1024)(128)(4,1)S(1)}, s32[]{:S(2)}) async-start(s8[4587520]{0:T(1024)(128)(4,1)} %bitcast.157), calls=%async_computation.16 | async-start | bytes 8388608
  687.2 8.5 slice-start.1
  702.6 358.2 %all-gather.15.cloned.1.call-start = ((), (), s32[]{:S(2)}) async-start(), calls=%async_computation.12 | async-start | bytes 15482880 | tf_op jit(solution)/shard_map/all_gather | solution.py:322
  703.2 452.1 %all-reduce.6.cloned.1.call-start = ((), (), s32[]{:S(2)}) async-start(), calls=%async_computation.11 | async-start | bytes 8060928 | tf_op jit(solution)/shard_map/psum | solution.py:323
  (47 other events, 121.6 us)
Sparse Core Ops, SparseCore 0:
  12.5 104.9 all-gather.6
  119.3 102.1 all-gather.8
  223.7 60.3 all-gather.10
  286.1 59.4 all-gather.12
  468.8 62.9 reduce-scatter.13
  534.0 58.2 reduce-scatter.11
  595.3 73.4 reduce-scatter.17
  672.0 127.5 reduce-scatter.15
  802.7 130.2 reduce-scatter.19
  934.5 126.3 all-gather.14
  1063.3 91.9 all-reduce.5
